TPU v7x, 32 devices: a whole 2x2x4 slice. The times are simulated.
32 devices in a mesh: tok: 8 (over z, x), tp: 4 (over y, core).
Axes of the slice: x: 2, y: 2, z: 4, core: 2. Of those that a mesh axis runs over, the one named last changes fastest.
Arguments:
- tokens: bfloat16 [36928, 768], P('tok'), may hold values from -6 to 6
- slot_index: int32 [36928], P('tok'), may hold values from -1 to 18477, as said below
- segment: int32 [36928], P('tok'), may hold values from 0 to 3, as said below
- router: float32 [768], replicated, may hold values from -0.21875 to 0.21875
- first_norm: float32 [2, 768], replicated, may hold values from -0.6 to 1.3
- qkv_weight: bfloat16 [768, 3, 768], P(None, None, 'tp'), may hold values from -0.21875 to 0.21875
- qv_bias: float32 [2, 768], P(None, 'tp'), may hold values from -4 to 4
- out_weight: bfloat16 [768, 768], P('tp'), may hold values from -1.75 to 1.75
- out_bias: float32 [768], P('tp'), may hold values from -4 to 4
- second_norm: float32 [2, 768], replicated, may hold values from -0.6 to 1.3
- up_weight: bfloat16 [768, 3072], P(None, 'tp'), may hold values from -0.21875 to 0.21875
- up_bias: float32 [3072], P('tp'), may hold values from -4 to 4
- down_weight: bfloat16 [3072, 768], P('tp'), may hold values from -0.109375 to 0.109375
- down_bias: float32 [768], P('tp'), may hold values from -4 to 4
- cotangent: bfloat16 [36928, 768], P('tok'), may hold values from -6 to 6
Outputs:
- layer_out: bfloat16 [36928, 768], P('tok', 'tp')
- d_tokens: float32 [36928, 768], P('tok', 'tp')
- d_qkv_weight: float32 [768, 3, 768], P(None, None, 'tp')
- d_qv_bias: float32 [2, 768], P(None, 'tp')
- d_out_weight: float32 [768, 768], P('tp')
- d_out_bias: float32 [768], P('tp')
- d_up_weight: float32 [768, 3072], P(None, 'tp')
- d_up_bias: float32 [3072], P('tp')
- d_down_weight: float32 [3072, 768], P('tp')
- d_down_bias: float32 [768], P('tp')
- d_first_norm: float32 [2, 768], P(None, 'tp')
- d_second_norm: float32 [2, 768], P(None, 'tp')
- d_router: float32 [768], P('tp')
Inputs may be any that keep to these rules, and one draw needn't show every extreme that they name: `slot_index`: -1 where the router leaves a patch out; else a slot of the compact buffers, slot // 289 being its row buffer, owned by index slot // 2312 of tok. No slot is named twice, each buffer's named slots are its lowest ones, every index of tok holds exactly 2168 selected patches and owns 2168 named slots, and at most 271 of the selected patches of one index of tok lie in rows of one owner. `segment`: within a row buffer the segments of named slots never fall from one slot to the next.
All inputs are finite; a program needn't handle non-finite values.
Results may differ from a plain program's by a relative error of at most 0.013.
Values may be sent and summed in bfloat16 or wider, within the bound.
No kernel may reach another device: no remote copies, remote signals or barrier semaphores. Data moves between devices by JAX's collectives and lax.ppermute only.
A program may use at most 320 MiB of HBM per device.

v0:
```python
import jax
import jax.numpy as jnp
from jax import lax
from jax.sharding import PartitionSpec as P

HD = 64
ROWS_DEV = 8
SLOTS = 289
EPSILON = 1e-06
MASKED_SCORE = -1000000000.0
BF = jnp.bfloat16
F32 = jnp.float32
EXACT = lax.Precision.HIGHEST


def ceil_to(value, step):
    return -(-value // step) * step


def normal_parts(values):
    row_mean = jnp.mean(values, axis=-1, keepdims=True)
    centered = values - row_mean
    inverse = lax.rsqrt(jnp.mean(centered * centered, axis=-1, keepdims=True) + EPSILON)
    return (centered * inverse, inverse)


def norm_back(grad_in, normal, inverse, gain_row):
    scaled = grad_in * gain_row
    return inverse * (
        scaled
        - jnp.mean(scaled, axis=-1, keepdims=True)
        - normal * jnp.mean(scaled * normal, axis=-1, keepdims=True)
    )


def mul(left, right):
    return lax.dot_general(left, right, (((1,), (0,)), ((), ())), preferred_element_type=F32)


def mul_t0(left, right):
    return lax.dot_general(left, right, (((0,), (0,)), ((), ())), preferred_element_type=F32)


def mul_t1(left, right):
    return lax.dot_general(left, right, (((1,), (1,)), ((), ())), preferred_element_type=F32)


def hot(rows, cols):
    return (rows[:, None] == cols[None, :]).astype(BF)


def columns_of(source, part, shares):
    width = source.shape[-1] // shares
    return lax.dynamic_slice_in_dim(source, part * width, width, source.ndim - 1)


def body(
    tokens,
    slot_index,
    segment,
    router,
    first_norm,
    qkv_weight,
    qv_bias,
    out_weight,
    out_bias,
    second_norm,
    up_weight,
    up_bias,
    down_weight,
    down_bias,
    cotangent,
):
    peers = lax.axis_size("tok")
    shares = lax.axis_size("tp")
    part = lax.axis_index("tp")
    half_bit = part % 2
    pair_bit = part // 2
    half_swap = [(i, i ^ 1) for i in range(shares)]
    pair_swap = [(i, i ^ 2) for i in range(shares)]
    count, width = tokens.shape
    inner = qkv_weight.shape[2]
    heads_local = inner // HD
    owned = ROWS_DEV * SLOTS
    live = owned - owned // 16
    capacity = -(-live // peers)
    quarter = -(-capacity // shares)
    block = ceil_to(quarter + 1, 8)
    picked = peers * block
    idle_share = -(-(count - live) // shares)
    idle = ceil_to(idle_share, 16)
    own = picked + idle
    chosen = slot_index >= 0
    owner = jnp.where(chosen, slot_index // owned, peers)
    lanes = jnp.arange(peers, dtype=jnp.int32)
    match = (owner[:, None] == lanes[None, :]).astype(jnp.int32)
    rank = jnp.sum(jnp.cumsum(match, axis=0) * match, axis=1) - 1
    idle_rank = jnp.cumsum(jnp.where(chosen, 0, 1)) - 1
    piece = rank // quarter
    offset = rank % quarter
    mine = chosen & (piece % 2 == half_bit)
    far = piece // 2 ^ pair_bit
    send_row = jnp.where(mine, (owner * 2 + far) * block + offset, -1)
    picked_row = jnp.where(mine & (far == 0), owner * block + offset, -1)
    own_row = jnp.where(
        chosen,
        picked_row,
        jnp.where(idle_rank // idle_share == part, picked + idle_rank % idle_share, -1),
    )
    back_picked = jnp.where(chosen, piece * picked + owner * block + offset, -1)
    back_idle = jnp.where(chosen, -1, idle_rank // idle_share * idle + idle_rank % idle_share)
    up_all = lax.all_gather(up_weight, "tp")
    down_all = lax.all_gather(down_weight, "tp")
    send_hot = hot(jnp.arange(2 * picked, dtype=jnp.int32), send_row)
    own_hot = hot(jnp.arange(own, dtype=jnp.int32), own_row)
    send_in = mul(send_hot, tokens)
    send_hat, _ = normal_parts(send_in)
    send_rows = (send_hat * first_norm[0] + first_norm[1]).astype(BF)
    local_slot = jnp.where(chosen, slot_index % owned, 0)
    marks = jnp.stack([local_slot // 64 + 1, local_slot % 64, segment])
    block_of = jnp.where(mine, owner * 2 + far, -1)
    block_hot = jnp.arange(2 * peers, dtype=jnp.int32)[:, None] == block_of[None, :]
    mark_left = jnp.where(block_hot[None], marks[:, None, :], 0).astype(BF)
    mark_right = hot(offset, jnp.arange(128, dtype=jnp.int32))
    mark_rows = mul(mark_left.reshape(6 * peers, count), mark_right).astype(BF)
    mark_rows = mark_rows.reshape(3, 2 * peers, 128).transpose(1, 0, 2).reshape(2 * peers, 1, 384)
    mark_rows = jnp.pad(mark_rows, ((0, 0), (0, 0), (0, width - 384)))
    row_kind = jnp.arange(block, dtype=jnp.int32)[None, :, None] == quarter
    send_rows = jnp.where(row_kind, mark_rows, send_rows.reshape(2 * peers, block, width))
    got_near = lax.all_to_all(
        send_rows.reshape(peers, 2, block, width), "tok", split_axis=0, concat_axis=0, tiled=True
    )
    got_far = lax.ppermute(got_near, "tp", half_swap)
    got = jnp.stack([got_near, got_far])
    mark = got[:, :, :, quarter, :].astype(jnp.int32)
    recv_slot = (mark[..., 0:block] - 1) * 64 + mark[..., 128 : 128 + block]
    recv_segment = mark[..., 256 : 256 + block]
    slot_rows = recv_slot.transpose(0, 2, 1, 3).reshape(4 * picked)
    segment_rows = recv_segment.transpose(0, 2, 1, 3).reshape(4 * picked)
    features = got.transpose(0, 2, 1, 3, 4).reshape(4 * picked, width)
    pad = 304
    ids = jnp.arange(ROWS_DEV * pad, dtype=jnp.int32)
    slot_ids = jnp.where(ids % pad < SLOTS, ids // pad * SLOTS + ids % pad, -1000)
    slot_hot = hot(slot_ids, slot_rows)
    slot_features = mul(slot_hot, features).astype(BF)
    flat_weight = qkv_weight.reshape(width, 3 * inner)
    bias_row = jnp.concatenate([qv_bias[0], jnp.zeros_like(qv_bias[0]), qv_bias[1]])
    slot_qkv = (mul(slot_features, flat_weight) + bias_row).astype(BF)
    slot_segment = (
        jnp.sum(jnp.where(slot_hot > 0, segment_rows[None, :] + 1, 0), axis=1) - 1
    ).reshape(ROWS_DEV, pad)
    allowed = (slot_segment[:, :, None] == slot_segment[:, None, :]) & (
        slot_segment[:, None, :] >= 0
    )
    grouped = slot_qkv.reshape(ROWS_DEV, pad, 3, heads_local, HD)
    query, key, value = (grouped[:, :, 0], grouped[:, :, 1], grouped[:, :, 2])
    score_scale = HD ** (-0.5)
    scores = jnp.einsum("rqhe,rkhe->rhqk", query, key, preferred_element_type=F32) * score_scale
    scores = jnp.where(allowed[:, None], scores, MASKED_SCORE)
    top = jnp.max(scores, axis=-1, keepdims=True)
    raised = jnp.exp(scores - top)
    weights = raised / jnp.sum(raised, axis=-1, keepdims=True)
    weights_low = weights.astype(BF)
    attended = jnp.einsum("rhqk,rkhe->rqhe", weights_low, value, preferred_element_type=F32)
    heads = attended.reshape(ROWS_DEV * pad, inner).astype(BF)
    heads_rows = mul_t0(slot_hot, heads).astype(BF)
    bias_full = lax.dynamic_update_slice(
        jnp.zeros((width,), F32), out_bias, (part * (width // shares),)
    )

    def share_sum(partial):
        near, far_half = (partial[: 2 * picked], partial[2 * picked :])
        got_half = lax.ppermute(far_half.astype(BF), "tp", half_swap)
        joined = near + got_half.astype(F32)
        got_pair = lax.ppermute(joined[picked:].astype(BF), "tp", pair_swap)
        return (joined[:picked] + got_pair.astype(F32)).astype(BF)

    def across(rows):
        return lax.all_to_all(
            rows.reshape(peers, block, width), "tok", split_axis=0, concat_axis=0, tiled=True
        ).reshape(picked, width)

    returned = across(share_sum(mul(heads_rows, out_weight) + bias_full))
    own_in = mul(own_hot, tokens)
    own_cot_low = mul(own_hot, cotangent).astype(BF)
    own_cot = own_cot_low.astype(F32)
    gate = jax.nn.sigmoid(jnp.dot(own_in, router, precision=EXACT))
    branch = jnp.pad(returned.astype(F32), ((0, idle), (0, 0)))
    scale = jnp.where(jnp.arange(own) < picked, gate, 0.0)
    residual = own_in + scale[:, None] * branch
    second_hat, second_inv = normal_parts(residual)
    second = (second_hat * second_norm[0] + second_norm[1]).astype(BF)
    up_cols = up_all.transpose(1, 0, 2).reshape(width, -1)
    down_rows = down_all.reshape(-1, width)
    up_bias_all = lax.all_gather(up_bias, "tp", tiled=True)
    down_bias_all = lax.all_gather(down_bias, "tp", tiled=True)
    pre = mul(second, up_cols) + up_bias_all
    below = 0.5 * (1.0 + lax.erf(pre * 2.0 ** (-0.5)))
    bell = jnp.exp(-0.5 * pre * pre) * (2.0 * jnp.pi) ** (-0.5)
    hidden = (pre * below).astype(BF)
    layer_rows = (residual + mul(hidden, down_rows) + down_bias_all).astype(BF)
    d_hidden = mul_t1(own_cot_low, down_rows)
    d_pre = (d_hidden * (below + pre * bell)).astype(BF)
    d_down = mul_t0(hidden, own_cot_low).astype(BF).reshape(shares, -1, width)
    d_up = mul_t0(second, d_pre).astype(BF)
    d_up = d_up.reshape(width, shares, -1).transpose(1, 0, 2)
    d_second = mul_t1(d_pre, up_cols)
    d_residual = own_cot + norm_back(d_second, second_hat, second_inv, second_norm[0])
    d_branch = (d_residual[:picked] * scale[:picked, None]).astype(BF)
    d_logit = jnp.sum(d_residual * branch, axis=1) * scale * (1.0 - gate)
    small = jnp.concatenate(
        [
            jnp.sum(d_pre.astype(F32), axis=0).reshape(shares, width),
            jnp.stack(
                [
                    jnp.sum(d_second * second_hat, axis=0),
                    jnp.sum(d_second, axis=0),
                    jnp.sum(own_cot, axis=0),
                    jnp.sum(d_branch.astype(F32), axis=0),
                    jnp.sum(d_logit[:, None] * own_in, axis=0),
                ]
            ),
        ]
    )
    d_up_share = lax.psum_scatter(d_up, "tp", scatter_dimension=0)
    d_down_share = lax.psum_scatter(d_down, "tp", scatter_dimension=0)
    d_up_total = lax.psum(d_up_share, "tok").astype(F32)
    d_down_total = lax.psum(d_down_share, "tok").astype(F32)
    grad_own = across(d_branch)
    grad_near = jnp.concatenate([grad_own, lax.ppermute(grad_own, "tp", pair_swap)])
    grad_rows = jnp.concatenate([grad_near, lax.ppermute(grad_near, "tp", half_swap)])
    d_out_weight = mul_t0(heads_rows, grad_rows)
    d_heads_rows = mul_t1(grad_rows, out_weight).astype(BF)
    d_heads = mul(slot_hot, d_heads_rows).astype(BF).reshape(ROWS_DEV, pad, heads_local, HD)
    d_weights = jnp.einsum("rqhe,rkhe->rhqk", d_heads, value, preferred_element_type=F32)
    d_value = jnp.einsum("rhqk,rqhe->rkhe", weights_low, d_heads, preferred_element_type=F32)
    d_scores = (
        weights * (d_weights - jnp.sum(weights * d_weights, axis=-1, keepdims=True))
    ).astype(BF)
    d_query = jnp.einsum("rhqk,rkhe->rqhe", d_scores, key, preferred_element_type=F32) * score_scale
    d_key = jnp.einsum("rhqk,rqhe->rkhe", d_scores, query, preferred_element_type=F32) * score_scale
    d_qkv = (
        jnp.stack([d_query, d_key, d_value], axis=2).astype(BF).reshape(ROWS_DEV * pad, 3 * inner)
    )
    d_qkv_weight = mul_t0(slot_features, d_qkv)
    d_qkv_bias = jnp.sum(d_qkv.astype(F32), axis=0).reshape(3, inner)
    d_qv_bias = jnp.stack([d_qkv_bias[0], d_qkv_bias[2]])
    d_qkv_rows = mul_t0(slot_hot, d_qkv).astype(BF)
    d_normed = across(share_sum(mul_t1(d_qkv_rows, flat_weight))).astype(F32)
    d_qkv_total = lax.psum(d_qkv_weight.astype(BF), "tok").astype(F32)
    d_out_total = lax.psum(d_out_weight.astype(BF), "tok").astype(F32)
    first_hat, first_inv = normal_parts(own_in[:picked])
    d_picked = (
        d_residual[:picked]
        + norm_back(d_normed, first_hat, first_inv, first_norm[0])
        + d_logit[:picked, None] * router[None, :]
    ).astype(BF)
    d_idle = d_residual[picked:].astype(BF)

    def to_columns(rows):
        pieces = rows.reshape(rows.shape[0], shares, width // shares).transpose(1, 0, 2)
        return lax.all_to_all(pieces, "tp", split_axis=0, concat_axis=0, tiled=True).reshape(
            shares * rows.shape[0], width // shares
        )

    picked_hot = hot(back_picked, jnp.arange(shares * picked, dtype=jnp.int32))
    idle_hot = hot(back_idle, jnp.arange(shares * idle, dtype=jnp.int32))
    layer_out = (
        mul(picked_hot, to_columns(layer_rows[:picked]))
        + mul(idle_hot, to_columns(layer_rows[picked:]))
    ).astype(BF)
    d_tokens = mul(picked_hot, to_columns(d_picked)) + mul(idle_hot, to_columns(d_idle))
    first_pair = jnp.stack([jnp.sum(d_normed * first_hat, axis=0), jnp.sum(d_normed, axis=0)])
    small = lax.psum(jnp.concatenate([small, first_pair]), ("tok", "tp"))
    small_cols = columns_of(small[shares:], part, shares)
    d_up_bias = lax.dynamic_slice_in_dim(small, part, 1, 0).reshape(width)
    d_qv_bias = lax.psum(d_qv_bias, "tok")
    return (
        layer_out,
        d_tokens,
        d_qkv_total.reshape(width, 3, inner),
        d_qv_bias,
        d_out_total,
        small_cols[3],
        d_up_total,
        d_up_bias,
        d_down_total,
        small_cols[2],
        small_cols[5:7],
        small_cols[0:2],
        small_cols[4],
    )


def solution(mesh):
    return jax.shard_map(
        body,
        mesh=mesh,
        in_specs=(
            P("tok", None),
            P("tok"),
            P("tok"),
            P(),
            P(),
            P(None, None, "tp"),
            P(None, "tp"),
            P("tp", None),
            P("tp"),
            P(),
            P(None, "tp"),
            P("tp"),
            P("tp", None),
            P("tp"),
            P("tok", None),
        ),
        out_specs=(
            P("tok", "tp"),
            P("tok", "tp"),
            P(None, None, "tp"),
            P(None, "tp"),
            P("tp", None),
            P("tp"),
            P(None, "tp"),
            P("tp"),
            P("tp", None),
            P("tp"),
            P(None, "tp"),
            P(None, "tp"),
            P("tp"),
        ),
        check_vma=False,
    )
```

profile of v0, /device:TPU:0, one launch (start us, length us, event | category | flops | bytes accessed | tf_op | source)
XLA Modules:
  0.0 696.7 jit_solution(4545855774942127467)
XLA Ops:
  16.0 14.7 %fusion.135 = (f32[1152]{0:T(1024)S(1)}, f32[1152,768]{1,0:T(8,128)S(1)}) fusion(bf16[4616,768]{1,0:T(8,128)(2,1)} %param.15, s32[4616]{0:T(1024)S(1)} %get-tuple-element.46), kind=kOutput, calls=%fused_computation.269 | convolution fusion | flops 8174084096 | bytes 10652192 | tf_op jit(solution)/shard_map/dot_general | solution.py:37
  32.1 48.4 %all_to_all.40 = bf16[8,2,72,768]{3,2,1,0:T(8,128)(2,1)S(1)} all-to-all(bf16[8,2,72,768]{3,2,1,0:T(8,128)(2,1)S(1)} %broadcast_select_fusion), channel_id=1, replica_groups=mesh['tok'=8,'tp'=4] {'tok'}, dimensions={0} | all-to-all | bytes 3538944 | tf_op jit(solution)/shard_map/all_to_all | solution.py:130
  81.6 2.9 collective-permute-done
  85.6 3.9 pad_maximum_fusion
  89.7 12.9 %fusion.44 = bf16[2432,768]{1,0:T(8,128)(2,1)} fusion(bf16[2304,768]{1,0:T(8,128)(2,1)} %bitcast.217, s32[2304]{0:T(1024)S(1)} %eq.201, s32[2432]{0:T(1024)S(1)} %fusion.120), kind=kOutput, calls=%fused_computation.64 | convolution fusion | flops 8614182912 | bytes 7293440 | tf_op jit(solution)/shard_map/dot_general | solution.py:37
  102.6 3.8 select_reduce_fusion
  106.5 6.2 add_convert_fusion
  112.7 7.5 %reshape.344 = bf16[8,304,3,3,64]{1,0,4,3,2:T(8,128)(2,1)} reshape(bf16[2432,576]{0,1:T(8,128)(2,1)} %add_convert_fusion) | data formatting | bytes 5603328 | tf_op jit(solution)/shard_map/reshape | solution.py:155
  122.3 3.4 fusion.131
  125.7 8.3 %fusion.136 = (f32[8,3,304]{2,1,0:T(4,128)S(1)}, f32[8,3,304,304]{2,3,1,0:T(8,128)}) fusion(pred[8,304,304]{1,2,0:T(8,128)(4,1)} %compare_and_fusion, bf16[8,304,1,3,64]{1,0,4,3,2:T(8,128)(2,1)S(1)} %get-tuple-element.38, bf16[8,304,1,3,64]{1,0,4,3,2:T(8,128)(2,1)S(1)} %get-tuple-element.37), kind=kOutput, calls=%fused_computation.270 | convolution fusion | flops 292774176 | bytes 11508224 | tf_op jit(solution)/shard_map/sub | solution.py:161
  134.0 5.8 fusion.83
  141.4 4.1 fusion.53
  146.7 2.9 copy-done.4
  150.0 3.7 collective-permute-done.1
  153.7 3.3 slice_add_fusion.1
  158.5 15.1 %fusion.16 = f32[1200,768]{1,0:T(8,128)S(1)} fusion(bf16[4616,768]{1,0:T(8,128)(2,1)} %param.15, s32[4616]{0:T(1024)S(1)} %get-tuple-element.47), kind=kOutput, calls=%fused_computation.20 | convolution fusion | flops 8513750528 | bytes 10795040 | tf_op jit(solution)/shard_map/dot_general | solution.py:37
  175.6 3.2 convolution_reduce_fusion
  178.8 20.2 %all-gather.2 = f32[4,1,768]{2,1,0:T(1,128)S(1)} all-gather(f32[1,1,768]{2,1,0:T(1,128)S(1)} %reshape.375), channel_id=1, replica_groups=mesh['tok'=8,'tp'=4] {'tp'}, dimensions={0}, use_global_device_ids=true | all-gather | bytes 15360 | tf_op jit(solution)/shard_map/all_gather | solution.py:195
  200.2 3.6 all-to-all-start.1
  203.8 14.8 %fusion.65 = bf16[1200,768]{1,0:T(8,128)(2,1)} fusion(bf16[4616,768]{1,0:T(8,128)(2,1)} %param.29, s32[4616]{0:T(1024)S(1)} %get-tuple-element.47), kind=kOutput, calls=%fused_computation.100 | convolution fusion | flops 8514672128 | bytes 8951840 | tf_op jit(solution)/shard_map/dot_general | solution.py:37
  218.6 6.6 copy.121
  226.7 2.8 fusion.130
  231.2 10.5 %multiply_convert_fusion = (bf16[1200,3072]{1,0:T(8,128)(2,1)S(1)}, f32[1200,3072]{1,0:T(8,128)}) fusion(f32[3072]{0:T(1024)S(1)} %bitcast.228, bf16[768,3072]{0,1:T(8,128)(2,1)S(1)} %bitcast.209, f32[768]{0:T(1024)S(1)} %get-tuple-element.24, f32[768]{0:T(1024)S(1)} %get-tuple-element.23, f32[1200]{0:T(1024)S(1)} %add_rsqrt_fusion, ...), kind=kOutput, calls=%fused_computation.34 | convolution fusion | flops 5691801600 | bytes 31440960 | tf_op jit(solution)/shard_map/dot_general | solution.py:37
  241.7 8.3 %convolution_convert_fusion = bf16[3072,768]{1,0:T(8,128)(2,1)} fusion(bf16[1200,3072]{1,0:T(8,128)(2,1)S(1)} %get-tuple-element.67, bf16[1200,768]{1,0:T(8,128)(2,1)S(1)} %copy-done.16), kind=kOutput, calls=%fused_computation.65 | convolution fusion | flops 5664669696 | bytes 13934592 | tf_op jit(solution)/shard_map/dot_general | solution.py:41
  250.2 14.4 %convert_reduce_fusion = (f32[3072]{0:T(1024)}, bf16[1200,3072]{1,0:T(8,128)(2,1)S(1)}) fusion(f32[1200,3072]{1,0:T(8,128)} %get-tuple-element.68, bf16[1200,768]{1,0:T(8,128)(2,1)} %fusion.65, bf16[3072,768]{1,0:T(8,128)(2,1)} %all-gather.8.cloned.1.call-done), kind=kOutput, calls=%fused_computation.33 | convolution fusion | flops 5706544128 | bytes 28692480 | tf_op jit(solution)/shard_map/dot_general | solution.py:45
  264.6 13.4 %multiply_reduce_fusion.2 = (f32[768]{0:T(1024)}, f32[1200]{0:T(1024)S(1)}, f32[1200]{0:T(1024)S(1)}, f32[768]{0:T(1024)}, f32[1200,768]{1,0:T(8,128)S(1)}) fusion(f32[1200]{0:T(1024)S(1)} %add_rsqrt_fusion, f32[1200]{0:T(1024)S(1)} %broadcast_multiply_fusion.2, f32[1200,768]{1,0:T(8,128)S(1)} %copy-done.3, bf16[576,768]{1,0:T(8,128)(2,1)S(1)} %bitcast.199, ...), kind=kOutput, calls=%fused_computation.86 | convolution fusion | flops 5673365504 | bytes 20382144 | tf_op jit(solution)/shard_map/dot_general | solution.py:45
  278.0 4.2 fusion.60
  284.8 27.2 %all_to_all.41 = bf16[8,72,768]{2,1,0:T(8,128)(2,1)S(1)} all-to-all(bf16[8,72,768]{2,1,0:T(8,128)(2,1)S(1)} %bitcast.218), channel_id=1, replica_groups=mesh['tok'=8,'tp'=4] {'tok'}, dimensions={0} | all-to-all | bytes 1769472 | tf_op jit(solution)/shard_map/all_to_all | solution.py:179
  317.4 17.7 %all-reduce.4 = f32[768]{0:T(1024)} all-reduce(f32[768]{0:T(1024)} %dynamic-update-slice), channel_id=1, replica_groups=mesh['tok'=8,'tp'=4] {'tp'}, use_global_device_ids=true, to_apply=%add.4 | all-reduce | flops 768 | bytes 6144
  336.6 10.9 %convolution_convert_fusion.1 = bf16[768,3072]{1,0:T(8,128)(2,1)S(1)} fusion(bf16[1200,3072]{1,0:T(8,128)(2,1)} %copy-done.52, f32[768]{0:T(1024)} %copy-done.45, f32[768]{0:T(1024)} %copy-done.34, f32[1200]{0:T(1024)} %copy-done.31, f32[1200]{0:T(1024)S(1)} %broadcast_multiply_fusion.2, f32[1200,768]{1,0:T(8,128)} %copy-done.1, ...), kind=kOutput, calls=%fused_computation.66 | convolution fusion | flops 5672042496 | bytes 16683072 | tf_op jit(solution)/shard_map/dot_general | solution.py:41
  347.5 2.5 copy.186
  350.0 7.7 %fusion.56 = bf16[2432,192]{0,1:T(8,128)(2,1)} fusion(s32[2304]{0:T(1024)} %copy-done.39, s32[2432]{0:T(1024)} %copy-done.41, bf16[192,768]{1,0:T(8,128)(2,1)} %param.22, bf16[1152,768]{1,0:T(8,128)(2,1)} %collective-permute-done.4, bf16[576,768]{1,0:T(8,128)(2,1)S(1)} %collective-permute-done.3, bf16[576,768]{1,0:T(8,128)(2,1)S(1)} %bitcast.214), kind=kOutput, calls=%fused_computation.81 | convolution fusion | flops 2848284672 | bytes 4786688 | tf_op jit(solution)/shard_map/dot_general | solution.py:37
  357.8 2.6 reshape.354
  360.5 6.4 fusion.75
  366.8 8.9 %multiply_reduce_fusion = (f32[8,3,304]{2,1,0:T(4,128)S(1)}, f32[8,3,304,304]{2,3,1,0:T(8,128)}) fusion(f32[8,3,304,304]{2,3,1,0:T(8,128)} %get-tuple-element.66, f32[8,3,304]{2,1,0:T(4,128)S(1)} %copy-done.29, bf16[8,304,1,3,64]{1,0,4,3,2:T(8,128)(2,1)S(1)} %copy-done.18, bf16[8,304,3,64]{1,0,3,2:T(8,128)(2,1)S(1)} %reshape.354), kind=kOutput, calls=%fused_computation.40 | convolution fusion | flops 290548608 | bytes 19670016 | tf_op jit(solution)/shard_map/rqhe,rkhe->rhqk/dot_general | solution.py:235
  375.8 6.1 multiply_convert_fusion.1
  386.1 4.1 copy.131
  390.2 6.7 convert_element_type.200
  396.9 16.6 %fusion.62 = f32[2304,768]{1,0:T(8,128)} fusion(bf16[768,576]{0,1:T(8,128)(2,1)S(1)} %bitcast.192, bf16[2432,576]{0,1:T(8,128)(2,1)} %convert_element_type.200, s32[2304]{0:T(1024)S(1)} %copy-done.40, s32[2432]{0:T(1024)S(1)} %copy-done.42), kind=kOutput, calls=%fused_computation.98 | convolution fusion | flops 8500396032 | bytes 10783232 | tf_op jit(solution)/shard_map/dot_general | solution.py:45
  413.6 3.8 slice.288
  417.8 10.6 %fusion.64 = bf16[1200,768]{1,0:T(8,128)(2,1)S(1)} fusion(bf16[1200,3072]{1,0:T(8,128)(2,1)} %copy-done.54, bf16[3072,768]{1,0:T(8,128)(2,1)} %all-gather.8.cloned.1.call-done, f32[768]{0:T(1024)S(1)} %copy-done.49, f32[1200,768]{1,0:T(8,128)} %copy-done.1, bf16[576,768]{1,0:T(8,128)(2,1)S(1)} %bitcast.202, f32[1200]{0:T(1024)S(1)} %fusion.123), kind=kOutput, calls=%fused_computation.99 | convolution fusion | flops 5667840000 | bytes 18513600 | tf_op jit(solution)/shard_map/dot_general | solution.py:37
  431.0 3.5 all-to-all-start.2
  437.6 10.7 %all-to-all-done.2 = bf16[4,576,192]{1,2,0:T(8,128)(2,1)S(1)} async-done(((bf16[4,576,192]{1,2,0:T(8,128)(2,1)}), bf16[4,576,192]{1,2,0:T(8,128)(2,1)S(1)}, u32[]{:S(2)}, u32[]{:S(2)}) %all-to-all-start.2) | async-done | bytes 884768 | tf_op jit(solution)/shard_map/all_to_all | solution.py:262
  448.2 4.2 all-to-all-start.3
  462.2 4.1 all-to-all-done.3
  466.3 3.5 all-to-all-start.7
  469.8 2.9 copy.125
  472.7 2.7 reshape.351
  475.4 2.9 slice_add_fusion
  483.0 13.4 %fusion.2 = f32[4616,192]{0,1:T(8,128)} fusion(bf16[2496,192]{0,1:T(8,128)(2,1)} %reshape.351, s32[4616]{0:T(1024)S(1)} %copy-done.33), kind=kOutput, calls=%fused_computation.3 | convolution fusion | flops 4435791360 | bytes 4522016 | tf_op jit(solution)/shard_map/dot_general | solution.py:37
  496.5 6.8 collective-permute-done.6
  503.3 2.6 fusion.71
  505.9 4.7 all-to-all-start.5
  510.6 13.9 %fusion.40 = bf16[4616,192]{0,1:T(8,128)(2,1)} fusion(f32[4616,192]{0,1:T(8,128)} %fusion.2, bf16[2304,192]{0,1:T(8,128)(2,1)} %reshape.349, s32[4616]{0:T(1024)S(1)} %copy-done.32), kind=kOutput, calls=%fused_computation.57 | convolution fusion | flops 4096349184 | bytes 6220832 | tf_op jit(solution)/shard_map/dot_general | solution.py:37
  526.2 2.7 reshape.359
  529.0 4.0 fusion.86
  533.2 3.4 convolution_convert_fusion.3
  543.3 3.7 all-to-all-start.6
  547.0 13.5 %fusion.1 = f32[4616,192]{0,1:T(8,128)} fusion(bf16[2496,192]{0,1:T(8,128)(2,1)} %reshape.359, s32[4616]{0:T(1024)S(1)} %copy-done.33), kind=kOutput, calls=%fused_computation.2 | convolution fusion | flops 4435791360 | bytes 4522016 | tf_op jit(solution)/shard_map/dot_general | solution.py:37
  560.7 23.7 %psum.43 = f32[2,192]{1,0:T(2,128)} all-reduce(f32[2,192]{1,0:T(2,128)S(1)} %pad_maximum_fusion.8), channel_id=1, replica_groups=mesh['tok'=8,'tp'=4] {'tok'}, use_global_device_ids=true, to_apply=%region_22.23 | all-reduce | flops 384 | bytes 3072 | tf_op jit(solution)/shard_map/psum | solution.py:277
  584.4 38.3 %psum.45 = f32[11,768]{1,0:T(8,128)S(1)} all-reduce(f32[11,768]{1,0:T(8,128)S(1)} %concatenate.16), channel_id=1, replica_groups=mesh['tok'=8,'tp'=4] {'tok','tp'}, use_global_device_ids=true, to_apply=%region_32.33 | all-reduce | flops 8448 | bytes 67584 | tf_op jit(solution)/shard_map/psum | solution.py:274
  626.1 13.6 %fusion.39 = f32[4616,192]{0,1:T(8,128)} fusion(f32[4616,192]{0,1:T(8,128)} %fusion.1, bf16[2304,192]{0,1:T(8,128)(2,1)S(1)} %reshape.357, s32[4616]{0:T(1024)S(1)} %copy-done.32), kind=kOutput, calls=%fused_computation.56 | convolution fusion | flops 4095462912 | bytes 7993376 | tf_op jit(solution)/shard_map/dot_general | solution.py:37
  639.7 42.5 %all-reduce.8.cloned.1.call-done = (bf16[768,3,192]{0,2,1:T(8,128)(2,1)}, bf16[192,768]{1,0:T(8,128)(2,1)}, bf16[768,768]{1,0:T(8,128)(2,1)}, bf16[768,768]{1,0:T(8,128)(2,1)}) async-done(((bf16[768,3,192]{0,2,1:T(8,128)(2,1)}, bf16[192,768]{1,0:T(8,128)(2,1)}, bf16[768,768]{1,0:T(8,128)(2,1)}, bf16[768,768]{1,0:T(8,128)(2,1)}), (bf16[768,3,192]{0,2,1:T(8,128)(2,1)}, bf16[192,768]{1,0:T(8,128)(2,1)}, ...) | async-done | bytes 3538960 | tf_op jit(solution)/shard_map/psum | solution.py:250
  684.2 2.5 reshape.361
  (269 shorter events, 76.2 us)
Async XLA Ops:
  7.2 99.3 %copy-start = (bf16[768,3,192]{0,2,1:T(8,128)(2,1)S(1)}, bf16[768,3,192]{0,2,1:T(8,128)(2,1)}, u32[]{:S(2)}) copy-start(bf16[768,3,192]{0,2,1:T(8,128)(2,1)} %param.20) | copy-start | bytes 2654212
  7.2 211.4 %all-gather.6.cloned.1.call-start = ((), (), s32[]{:S(2)}) async-start(), calls=%async_computation.12 | async-start | bytes 5898240 | tf_op jit(solution)/shard_map/all_gather | solution.py:112
  8.1 23.2 %copy-start.23 = (f32[768]{0:T(1024)}, f32[768]{0:T(1024)S(1)}, u32[]{:S(2)}) copy-start(f32[768]{0:T(1024)S(1)} %get-tuple-element.21) | copy-start | bytes 9220
  32.1 49.1 %copy-start.51 = (f32[192]{0:T(256)S(1)}, f32[192]{0:T(256)}, u32[]{:S(2)}) copy-start(f32[192]{0:T(256)} %param.23) | copy-start | bytes 2308
  32.1 49.4 %copy-start.50 = (f32[2,192]{1,0:T(2,128)S(1)}, f32[2,192]{1,0:T(2,128)}, u32[]{:S(2)}) copy-start(f32[2,192]{1,0:T(2,128)} %param.21) | copy-start | bytes 4612
  80.6 3.9 collective-permute-start
  80.7 169.5 %all-gather.8.cloned.1.call-start = ((), (), s32[]{:S(2)}) async-start(), calls=%async_computation.13 | async-start | bytes 5898240 | tf_op jit(solution)/shard_map/all_gather | solution.py:113
  81.6 59.8 %copy-start.41 = (s32[2432]{0:T(1024)}, s32[2432]{0:T(1024)S(1)}, u32[]{:S(2)}) copy-start(s32[2432]{0:T(1024)S(1)} %fusion.120) | copy-start | bytes 29188
  89.7 51.7 %copy-start.39 = (s32[2304]{0:T(1024)}, s32[2304]{0:T(1024)S(1)}, u32[]{:S(2)}) copy-start(s32[2304]{0:T(1024)S(1)} %eq.201) | copy-start | bytes 27652
  125.7 8.3 %copy-start.7 = (bf16[8,304,1,3,64]{1,0,4,3,2:T(8,128)(2,1)}, bf16[8,304,1,3,64]{1,0,4,3,2:T(8,128)(2,1)S(1)}, u32[]{:S(2)}) copy-start(bf16[8,304,1,3,64]{1,0,4,3,2:T(8,128)(2,1)S(1)} %get-tuple-element.37) | copy-start | bytes 2801668
  125.7 8.3 %copy-start.10 = (bf16[8,304,1,3,64]{1,0,4,3,2:T(8,128)(2,1)}, bf16[8,304,1,3,64]{1,0,4,3,2:T(8,128)(2,1)S(1)}, u32[]{:S(2)}) copy-start(bf16[8,304,1,3,64]{1,0,4,3,2:T(8,128)(2,1)S(1)} %get-tuple-element.38) | copy-start | bytes 2801668
  134.0 5.8 copy-start.28
  149.8 3.9 collective-permute-start.1
  157.1 42.0 %collective-permute-start.2 = (bf16[576,768]{1,0:T(8,128)(2,1)S(1)}, bf16[576,768]{1,0:T(8,128)(2,1)S(1)}, u32[]{:S(2)}, u32[]{:S(2)}) collective-permute-start(bf16[576,768]{1,0:T(8,128)(2,1)S(1)} %slice.292), channel_id=1, source_target_pairs={{0,2},{1,3},{2,0},{3,1},{4,6},{5,7},{6,4},{7,5},{8,10},{9,11},{10,... | collective-permute-start | bytes 2654216 | tf_op jit(solution)/shard_map/ppermute | solution.py:175
  158.5 15.1 %copy-start.46 = (f32[768]{0:T(1024)S(1)}, f32[768]{0:T(1024)}, u32[]{:S(2)}) copy-start(f32[768]{0:T(1024)} %param.26) | copy-start | bytes 9220
  158.5 15.2 %copy-start.35 = (f32[768]{0:T(1024)S(1)}, f32[768]{0:T(1024)}, u32[]{:S(2)}) copy-start(f32[768]{0:T(1024)} %param.18) | copy-start | bytes 9220
  173.6 25.4 %copy-start.44 = (f32[2,768]{1,0:T(2,128)S(1)}, f32[2,768]{1,0:T(2,128)}, u32[]{:S(2)}) copy-start(f32[2,768]{1,0:T(2,128)} %param.24) | copy-start | bytes 18436
  178.8 21.4 %copy-start.25 = (f32[1200]{0:T(1024)}, f32[1200]{0:T(1024)S(1)}, u32[]{:S(2)}) copy-start(f32[1200]{0:T(1024)S(1)} %convolution_reduce_fusion) | copy-start | bytes 14404
  199.0 31.7 %copy-start.45 = (f32[768]{0:T(1024)}, f32[768]{0:T(1024)S(1)}, u32[]{:S(2)}) copy-start(f32[768]{0:T(1024)S(1)} %get-tuple-element.24) | copy-start | bytes 9220
  199.1 78.9 %copy-start.34 = (f32[768]{0:T(1024)}, f32[768]{0:T(1024)S(1)}, u32[]{:S(2)}) copy-start(f32[768]{0:T(1024)S(1)} %get-tuple-element.23) | copy-start | bytes 9220
  200.2 26.5 %all-to-all-start.1 = ((bf16[8,72,768]{2,1,0:T(8,128)(2,1)}), bf16[8,72,768]{2,1,0:T(8,128)(2,1)S(1)}, u32[]{:S(2)}, u32[]{:S(2)}) async-start(bf16[8,72,768]{2,1,0:T(8,128)(2,1)} %bitcast.21), calls=%async_computation.1 | async-start | bytes 1769472 | tf_op jit(solution)/shard_map/all_to_all | solution.py:179
  203.7 335.6 %reduce-scatter.5.cloned.1.call-start = ((), (), s32[]{:S(2)}) async-start(), calls=%async_computation.11 | async-start | bytes 5898240 | tf_op jit(solution)/shard_map/reduce_scatter | solution.py:226
  226.7 4.6 copy-start.9
  230.8 47.2 %copy-start.31 = (f32[1200]{0:T(1024)}, f32[1200]{0:T(1024)S(1)}, u32[]{:S(2)}) copy-start(f32[1200]{0:T(1024)S(1)} %add_rsqrt_fusion) | copy-start | bytes 14404
  231.2 10.5 %copy-start.16 = (bf16[1200,768]{1,0:T(8,128)(2,1)S(1)}, bf16[1200,768]{1,0:T(8,128)(2,1)}, u32[]{:S(2)}) copy-start(bf16[1200,768]{1,0:T(8,128)(2,1)} %fusion.65) | copy-start | bytes 5529604
  241.7 8.3 %copy-start.54 = (bf16[1200,3072]{1,0:T(8,128)(2,1)}, bf16[1200,3072]{1,0:T(8,128)(2,1)S(1)}, u32[]{:S(2)}) copy-start(bf16[1200,3072]{1,0:T(8,128)(2,1)S(1)} %get-tuple-element.67) | copy-start | bytes 22118404
  250.1 289.3 %reduce-scatter.3.cloned.1.call-start = ((), (), s32[]{:S(2)}) async-start(), calls=%async_computation.10 | async-start | bytes 5898240 | tf_op jit(solution)/shard_map/reduce_scatter | solution.py:225
  250.2 14.4 %copy-start.3 = (f32[1200,768]{1,0:T(8,128)S(1)}, f32[1200,768]{1,0:T(8,128)}, u32[]{:S(2)}) copy-start(f32[1200,768]{1,0:T(8,128)} %copy-done.1) | copy-start | bytes 11059204
  264.5 13.4 %copy-start.52 = (bf16[1200,3072]{1,0:T(8,128)(2,1)}, bf16[1200,3072]{1,0:T(8,128)(2,1)S(1)}, u32[]{:S(2)}) copy-start(bf16[1200,3072]{1,0:T(8,128)(2,1)S(1)} %get-tuple-element.73) | copy-start | bytes 22118404
  264.6 13.5 %copy-start.17 = (bf16[1200,768]{1,0:T(8,128)(2,1)S(1)}, bf16[1200,768]{1,0:T(8,128)(2,1)}, u32[]{:S(2)}) copy-start(bf16[1200,768]{1,0:T(8,128)(2,1)} %fusion.65) | copy-start | bytes 5529604
  312.0 38.1 %copy-start.13 = (bf16[8,72,768]{2,1,0:T(8,128)(2,1)}, bf16[8,72,768]{2,1,0:T(8,128)(2,1)S(1)}, u32[]{:S(2)}) copy-start(bf16[8,72,768]{2,1,0:T(8,128)(2,1)S(1)} %all_to_all.41) | copy-start | bytes 2654212
  312.0 23.2 %collective-permute-start.3 = (bf16[576,768]{1,0:T(8,128)(2,1)S(1)}, bf16[576,768]{1,0:T(8,128)(2,1)S(1)}, u32[]{:S(2)}, u32[]{:S(2)}) collective-permute-start(bf16[576,768]{1,0:T(8,128)(2,1)S(1)} %bitcast.212), channel_id=1, source_target_pairs={{0,2},{1,3},{2,0},{3,1},{4,6},{5,7},{6,4},{7,5},{8,10},{9,11},{10,... | collective-permute-start | bytes 2654216 | tf_op jit(solution)/shard_map/ppermute | solution.py:230
  335.2 14.9 %copy-start.21 = (bf16[576,768]{1,0:T(8,128)(2,1)}, bf16[576,768]{1,0:T(8,128)(2,1)S(1)}, u32[]{:S(2)}) copy-start(bf16[576,768]{1,0:T(8,128)(2,1)S(1)} %collective-permute-done.3) | copy-start | bytes 2654212
  336.6 13.4 %collective-permute-start.4 = (bf16[1152,768]{1,0:T(8,128)(2,1)}, bf16[1152,768]{1,0:T(8,128)(2,1)}, u32[]{:S(2)}, u32[]{:S(2)}) collective-permute-start(bf16[1152,768]{1,0:T(8,128)(2,1)} %pad_maximum_fusion.2), channel_id=1, source_target_pairs={{0,1},{1,0},{2,3},{3,2},{4,5},{5,4},{6,7},{7,6},{8,9},{9,8},{10,11... | collective-permute-start | bytes 5308424 | tf_op jit(solution)/shard_map/ppermute | solution.py:231
  360.4 6.4 copy-start.18
  360.4 6.4 copy-start.29
  360.4 15.3 %slice-start = ((s8[11206656]{0:T(1024)(128)(4,1)}), s8[4194304]{0:T(1024)(128)(4,1)S(1)}, s32[]{:S(2)}) async-start(s8[11206656]{0:T(1024)(128)(4,1)} %bitcast.203), calls=%async_computation.15 | async-start | bytes 8388608
  360.4 15.3 %slice-start.1 = ((s8[11206656]{0:T(1024)(128)(4,1)}), s8[4194304]{0:T(1024)(128)(4,1)S(1)}, s32[]{:S(2)}) async-start(s8[11206656]{0:T(1024)(128)(4,1)} %bitcast.203), calls=%async_computation.16 | async-start | bytes 8388608
  366.8 8.9 %slice-start.2 = ((s8[11206656]{0:T(1024)(128)(4,1)}), s8[2818048]{0:T(1024)(128)(4,1)S(1)}, s32[]{:S(2)}) async-start(s8[11206656]{0:T(1024)(128)(4,1)} %bitcast.203), calls=%async_computation.17 | async-start | bytes 5636096
  375.7 6.2 copy-start.11
  390.2 6.7 copy-start.40
  390.2 6.7 copy-start.42
  396.9 20.9 %copy-start.49 = (f32[768]{0:T(1024)S(1)}, f32[768]{0:T(1024)}, u32[]{:S(2)}) copy-start(f32[768]{0:T(1024)} %all-reduce.4) | copy-start | bytes 9220
  417.3 58.1 %collective-permute-start.5 = (bf16[1152,768]{1,0:T(8,128)(2,1)}, bf16[1152,768]{1,0:T(8,128)(2,1)}, u32[]{:S(2)}, u32[]{:S(2)}) collective-permute-start(bf16[1152,768]{1,0:T(8,128)(2,1)} %slice.288), channel_id=1, source_target_pairs={{0,1},{1,0},{2,3},{3,2},{4,5},{5,4},{6,7},{7,6},{8,9},{9,8},{10,11... | collective-permute-start | bytes 5308424 | tf_op jit(solution)/shard_map/ppermute | solution.py:173
  429.7 6.5 slice-start.3
  431.0 17.2 %all-to-all-start.2 = ((bf16[4,576,192]{1,2,0:T(8,128)(2,1)}), bf16[4,576,192]{1,2,0:T(8,128)(2,1)S(1)}, u32[]{:S(2)}, u32[]{:S(2)}) async-start(bf16[4,576,192]{1,2,0:T(8,128)(2,1)} %bitcast.29), calls=%async_computation.2 | async-start | bytes 1966080 | tf_op jit(solution)/shard_map/all_to_all | solution.py:262
  436.2 19.8 %copy-start.43 = (f32[3072]{0:T(1024)S(1)}, f32[3072]{0:T(1024)}, u32[]{:S(2)}) copy-start(f32[3072]{0:T(1024)} %get-tuple-element.72) | copy-start | bytes 36868
  436.2 19.8 %copy-start.48 = (f32[768]{0:T(1024)S(1)}, f32[768]{0:T(1024)}, u32[]{:S(2)}) copy-start(f32[768]{0:T(1024)} %get-tuple-element.13) | copy-start | bytes 9220
  436.2 19.8 %copy-start.47 = (f32[768]{0:T(1024)S(1)}, f32[768]{0:T(1024)}, u32[]{:S(2)}) copy-start(f32[768]{0:T(1024)} %get-tuple-element.18) | copy-start | bytes 9220
  436.2 19.8 %copy-start.38 = (f32[768]{0:T(1024)S(1)}, f32[768]{0:T(1024)}, u32[]{:S(2)}) copy-start(f32[768]{0:T(1024)} %get-tuple-element.40) | copy-start | bytes 9220
  436.2 19.8 %copy-start.26 = (f32[1200]{0:T(1024)S(1)}, f32[1200]{0:T(1024)}, u32[]{:S(2)}) copy-start(f32[1200]{0:T(1024)} %copy-done.25) | copy-start | bytes 14404
  436.2 19.8 %copy-start.30 = (f32[1200]{0:T(1024)S(1)}, f32[1200]{0:T(1024)}, u32[]{:S(2)}) copy-start(f32[1200]{0:T(1024)} %get-tuple-element.33) | copy-start | bytes 14404
  448.2 18.1 %all-to-all-start.3 = ((bf16[4,624,192]{1,2,0:T(8,128)(2,1)}), bf16[4,624,192]{1,2,0:T(8,128)(2,1)}, u32[]{:S(2)}, u32[]{:S(2)}) async-start(bf16[4,624,192]{1,2,0:T(8,128)(2,1)} %bitcast.31), calls=%async_computation.3 | async-start | bytes 1966080 | tf_op jit(solution)/shard_map/all_to_all | solution.py:262
  452.5 6.0 copy-start.37
  456.1 4.5 copy-start.27
  466.3 39.6 %all-to-all-start.7 = ((bf16[4,624,192]{1,2,0:T(8,128)(2,1)}), bf16[4,624,192]{1,2,0:T(8,128)(2,1)S(1)}, u32[]{:S(2)}, u32[]{:S(2)}) async-start(bf16[4,624,192]{1,2,0:T(8,128)(2,1)} %bitcast.211), calls=%async_computation.7 | async-start | bytes 1966080 | tf_op jit(solution)/shard_map/all_to_all | solution.py:262
  475.4 7.6 %copy-start.33 = (s32[4616]{0:T(1024)S(1)}, s32[4616]{0:T(1024)}, u32[]{:S(2)}) copy-start(s32[4616]{0:T(1024)} %get-tuple-element.49) | copy-start | bytes 55396
  481.1 22.2 %collective-permute-start.6 = (bf16[576,768]{1,0:T(8,128)(2,1)}, bf16[576,768]{1,0:T(8,128)(2,1)S(1)}, u32[]{:S(2)}, u32[]{:S(2)}) collective-permute-start(bf16[576,768]{1,0:T(8,128)(2,1)} %slice.291), channel_id=1, source_target_pairs={{0,2},{1,3},{2,0},{3,1},{4,6},{5,7},{6,4},{7,5},{8,10},{9,11},{10,... | collective-permute-start | bytes 2654216 | tf_op jit(solution)/shard_map/ppermute | solution.py:175
  496.5 14.1 %copy-start.32 = (s32[4616]{0:T(1024)S(1)}, s32[4616]{0:T(1024)}, u32[]{:S(2)}) copy-start(s32[4616]{0:T(1024)} %get-tuple-element.45) | copy-start | bytes 55396
  505.9 30.6 %all-to-all-start.5 = ((bf16[8,72,768]{2,1,0:T(8,128)(2,1)}), bf16[8,72,768]{2,1,0:T(8,128)(2,1)S(1)}, u32[]{:S(2)}, u32[]{:S(2)}) async-start(bf16[8,72,768]{2,1,0:T(8,128)(2,1)} %bitcast.216), calls=%async_computation.5 | async-start | bytes 1769472 | tf_op jit(solution)/shard_map/all_to_all | solution.py:179
  510.6 171.6 %all-reduce.8.cloned.1.call-start = ((), (), s32[]{:S(2)}) async-start(), calls=%async_computation.14 | async-start | bytes 7077888 | tf_op jit(solution)/shard_map/psum | solution.py:250
  543.3 81.4 %all-to-all-start.6 = ((bf16[4,576,192]{1,2,0:T(8,128)(2,1)}), bf16[4,576,192]{1,2,0:T(8,128)(2,1)S(1)}, u32[]{:S(2)}, u32[]{:S(2)}) async-start(bf16[4,576,192]{1,2,0:T(8,128)(2,1)} %bitcast.43), calls=%async_computation.6 | async-start | bytes 1966080 | tf_op jit(solution)/shard_map/all_to_all | solution.py:262
  682.2 4.5 copy-start.20
  682.2 6.1 copy-start.19
  (14 other events, 36.3 us)
Sparse Core Ops, SparseCore 0:
  80.8 36.5 all-gather.5
  150.1 55.4 all-gather.7
  250.2 47.7 reduce-scatter.4
  350.1 46.8 reduce-scatter.2
  539.5 142.6 all-reduce.7
where the time goes:
time: 705 us; the launch traced here: 697 us
  matrix products  260 us (37%)
  blocking collectives  175 us (25%)
  local copies, waits for them, and re-layouts  80 us (11%)
  waiting for transfers between devices  72.2 us (10%)
  other arithmetic  63.8 us (9%)
  starting transfers between devices  29.5 us (4%)
  between operations  16.1 us (2%)
    dot_general x14, matrix products, mul(): lax.dot_general(left, right, (((1,), (0,)), ((), ())), preferred_element_...  149 us
    all_to_all x1, blocking collectives, body(): lax.all_to_all(send_rows.reshape(peers, 2, block, width), 'tok', split_ax...  48.4 us
    dot_general x3, matrix products, mul_t1(): lax.dot_general(left, right, (((1,), (1,)), ((), ())), preferred_element_...  44.5 us
    psum x1, waiting for transfers between devices, body(): d_qkv_total = lax.psum(d_qkv_weight.astype(BF), 'tok').astype(F32)  42.5 us
    psum x1, blocking collectives, body(): small = lax.psum(jnp.concatenate([small, first_pair]), ('tok', 'tp'))  38.3 us
    dot_general x5, matrix products, mul_t0(): lax.dot_general(left, right, (((0,), (0,)), ((), ())), preferred_element_...  30.6 us
    all_to_all x1, blocking collectives, across(): lax.all_to_all(rows.reshape(peers, block, width), 'tok', split_axis=0, co...  27.2 us
    psum x1, blocking collectives, body(): d_qv_bias = lax.psum(d_qv_bias, 'tok')  23.7 us
  transfers between devices with their start and end apart: 18, of which 7 were waited for; matrix products, arithmetic and copies ran while one was open for 52% of the time, Pallas kernels for 0%

commit v1 on v0

--- a/solution.py
+++ b/solution.py
@@ -274,7 +274,11 @@
     small = lax.psum(jnp.concatenate([small, first_pair]), ("tok", "tp"))
     small_cols = columns_of(small[shares:], part, shares)
     d_up_bias = lax.dynamic_slice_in_dim(small, part, 1, 0).reshape(width)
-    d_qv_bias = lax.psum(d_qv_bias, "tok")
+    d_qv_bias = d_qv_bias
+    for hop in (1, 2, 4):
+        d_qv_bias = d_qv_bias + lax.ppermute(
+            d_qv_bias, "tok", [(dev, dev ^ hop) for dev in range(8)]
+        )
     return (
         layer_out,
         d_tokens,

time: 705 us -> 679 us (0.963)
  blocking collectives: 175 us -> 116 us
  waiting for transfers between devices: 72.2 us -> 92.6 us
  starting transfers between devices: 29.5 us -> 43.3 us
    all_to_all x1 -> x0, blocking collectives: 27.2 us -> none  [across(): lax.all_to_all(rows.reshape(peers, block, width), 'tok', split_axis=0, co...]
    psum x1 -> x0, blocking collectives: 23.7 us -> none  [body(): d_qv_bias = lax.psum(d_qv_bias, 'tok')]
    all_to_all x4, waiting for transfers between devices: 14.8 us -> 0.01 us  [to_columns(): lax.all_to_all(pieces, 'tp', split_axis=0, concat_axis=0, tiled=True)]
    psum x1, waiting for transfers between devices: 42.5 us -> 56.6 us  [body(): d_qkv_total = lax.psum(d_qkv_weight.astype(BF), 'tok').astype(F32)]
    all_to_all x2 -> x3, waiting for transfers between devices: 1.41 us -> 14.9 us  [across(): lax.all_to_all(rows.reshape(peers, block, width), 'tok', split_axis=0, co...]
    unnamed x1, blocking collectives: 17.7 us -> 6.65 us
    ppermute x0 -> x3, starting transfers between devices: none -> 8.18 us  [body(): lax.ppermute(d_qv_bias, 'tok', [(dev, dev ^ hop) for dev in range(8)])]
    ppermute x1, waiting for transfers between devices: 0.01 us -> 7.61 us  [body(): lax.ppermute(grad_own, 'tp', pair_swap)]
  transfers between devices with their start and end apart: 18 -> 22, of which waited for: 7 -> 9; matrix products, arithmetic and copies ran while one was open for 52% -> 54% of each run, Pallas kernels for 0% -> 0%
where the time goes in v1:
time: 679 us; the launch traced here: 670 us
  matrix products  261 us (38%)
  blocking collectives  116 us (17%)
  waiting for transfers between devices  92.6 us (14%)
  local copies, waits for them, and re-layouts  77.4 us (11%)
  other arithmetic  64.6 us (10%)
  starting transfers between devices  43.3 us (6%)
  between operations  16 us (2%)
    dot_general x14, matrix products, mul(): lax.dot_general(left, right, (((1,), (0,)), ((), ())), preferred_element_...  148 us
    psum x1, waiting for transfers between devices, body(): d_qkv_total = lax.psum(d_qkv_weight.astype(BF), 'tok').astype(F32)  56.6 us
    all_to_all x1, blocking collectives, body(): lax.all_to_all(send_rows.reshape(peers, 2, block, width), 'tok', split_ax...  48.4 us
    dot_general x3, matrix products, mul_t1(): lax.dot_general(left, right, (((1,), (1,)), ((), ())), preferred_element_...  44.3 us
    psum x1, blocking collectives, body(): small = lax.psum(jnp.concatenate([small, first_pair]), ('tok', 'tp'))  40.4 us
    dot_general x5, matrix products, mul_t0(): lax.dot_general(left, right, (((0,), (0,)), ((), ())), preferred_element_...  32 us
    all_gather x1, blocking collectives, body(): up_bias_all = lax.all_gather(up_bias, 'tp', tiled=True)  20.2 us
    all_to_all x4, starting transfers between devices, to_columns(): lax.all_to_all(pieces, 'tp', split_axis=0, concat_axis=0, tiled=True)  15.3 us
  transfers between devices with their start and end apart: 22, of which 9 were waited for; matrix products, arithmetic and copies ran while one was open for 54% of the time, Pallas kernels for 0%

profile of v1, /device:TPU:0, one launch (start us, length us, event | category | flops | bytes accessed | tf_op | source)
XLA Modules:
  0.0 670.3 jit_solution(3554169331562140585)
XLA Ops:
  16.0 14.7 %fusion.136 = (f32[1152]{0:T(1024)S(1)}, f32[1152,768]{1,0:T(8,128)S(1)}) fusion(bf16[4616,768]{1,0:T(8,128)(2,1)} %param.15, s32[4616]{0:T(1024)S(1)} %get-tuple-element.46), kind=kOutput, calls=%fused_computation.270 | convolution fusion | flops 8174084096 | bytes 10652192 | tf_op jit(solution)/shard_map/dot_general | solution.py:37
  32.1 48.4 %all_to_all.40 = bf16[8,2,72,768]{3,2,1,0:T(8,128)(2,1)S(1)} all-to-all(bf16[8,2,72,768]{3,2,1,0:T(8,128)(2,1)S(1)} %broadcast_select_fusion), channel_id=1, replica_groups=mesh['tok'=8,'tp'=4] {'tok'}, dimensions={0} | all-to-all | bytes 3538944 | tf_op jit(solution)/shard_map/all_to_all | solution.py:130
  81.6 2.9 collective-permute-done
  85.6 3.9 pad_maximum_fusion
  89.7 12.9 %fusion.44 = bf16[2432,768]{1,0:T(8,128)(2,1)} fusion(bf16[2304,768]{1,0:T(8,128)(2,1)} %bitcast.216, s32[2304]{0:T(1024)S(1)} %eq.201, s32[2432]{0:T(1024)S(1)} %fusion.120), kind=kOutput, calls=%fused_computation.64 | convolution fusion | flops 8614182912 | bytes 7293440 | tf_op jit(solution)/shard_map/dot_general | solution.py:37
  102.6 3.8 select_reduce_fusion
  106.5 6.1 add_convert_fusion
  112.6 7.5 %reshape.344 = bf16[8,304,3,3,64]{1,0,4,3,2:T(8,128)(2,1)} reshape(bf16[2432,576]{0,1:T(8,128)(2,1)} %add_convert_fusion) | data formatting | bytes 5603328 | tf_op jit(solution)/shard_map/reshape | solution.py:155
  122.2 3.4 fusion.132
  125.6 8.3 %fusion.137 = (f32[8,3,304]{2,1,0:T(4,128)S(1)}, f32[8,3,304,304]{2,3,1,0:T(8,128)}) fusion(pred[8,304,304]{1,2,0:T(8,128)(4,1)} %compare_and_fusion, bf16[8,304,1,3,64]{1,0,4,3,2:T(8,128)(2,1)S(1)} %get-tuple-element.38, bf16[8,304,1,3,64]{1,0,4,3,2:T(8,128)(2,1)S(1)} %get-tuple-element.37), kind=kOutput, calls=%fused_computation.271 | convolution fusion | flops 292774176 | bytes 11508224 | tf_op jit(solution)/shard_map/sub | solution.py:161
  134.0 5.8 fusion.83
  141.4 4.1 fusion.53
  146.7 2.9 copy-done.5
  149.9 3.7 collective-permute-done.1
  153.6 3.3 slice_add_fusion.1
  158.4 15.1 %fusion.16 = f32[1200,768]{1,0:T(8,128)S(1)} fusion(bf16[4616,768]{1,0:T(8,128)(2,1)} %param.15, s32[4616]{0:T(1024)S(1)} %copy-done.43), kind=kOutput, calls=%fused_computation.20 | convolution fusion | flops 8513750528 | bytes 10795040 | tf_op jit(solution)/shard_map/dot_general | solution.py:37
  175.4 3.2 convolution_reduce_fusion
  178.7 20.2 %all-gather.2 = f32[4,1,768]{2,1,0:T(1,128)S(1)} all-gather(f32[1,1,768]{2,1,0:T(1,128)S(1)} %reshape.375), channel_id=1, replica_groups=mesh['tok'=8,'tp'=4] {'tp'}, dimensions={0}, use_global_device_ids=true | all-gather | bytes 15360 | tf_op jit(solution)/shard_map/all_gather | solution.py:195
  200.0 3.6 all-to-all-start.1
  203.6 14.8 %fusion.65 = bf16[1200,768]{1,0:T(8,128)(2,1)} fusion(bf16[4616,768]{1,0:T(8,128)(2,1)} %param.29, s32[4616]{0:T(1024)S(1)} %copy-done.43), kind=kOutput, calls=%fused_computation.100 | convolution fusion | flops 8514672128 | bytes 8951840 | tf_op jit(solution)/shard_map/dot_general | solution.py:37
  218.5 6.6 copy.121
  226.5 2.8 fusion.131
  231.1 10.5 %multiply_convert_fusion = (bf16[1200,3072]{1,0:T(8,128)(2,1)S(1)}, f32[1200,3072]{1,0:T(8,128)}) fusion(f32[3072]{0:T(1024)S(1)} %bitcast.226, bf16[768,3072]{0,1:T(8,128)(2,1)S(1)} %bitcast.209, f32[768]{0:T(1024)S(1)} %get-tuple-element.24, f32[768]{0:T(1024)S(1)} %get-tuple-element.23, f32[1200]{0:T(1024)S(1)} %add_rsqrt_fusion, ...), kind=kOutput, calls=%fused_computation.34 | convolution fusion | flops 5691801600 | bytes 31440960 | tf_op jit(solution)/shard_map/dot_general | solution.py:37
  241.6 8.3 %convolution_convert_fusion = bf16[3072,768]{1,0:T(8,128)(2,1)} fusion(bf16[1200,3072]{1,0:T(8,128)(2,1)S(1)} %get-tuple-element.67, bf16[1200,768]{1,0:T(8,128)(2,1)S(1)} %copy-done.19), kind=kOutput, calls=%fused_computation.65 | convolution fusion | flops 5664669696 | bytes 13934592 | tf_op jit(solution)/shard_map/dot_general | solution.py:41
  250.0 14.4 %convert_reduce_fusion = (f32[3072]{0:T(1024)}, bf16[1200,3072]{1,0:T(8,128)(2,1)S(1)}) fusion(f32[1200,3072]{1,0:T(8,128)} %get-tuple-element.68, bf16[1200,768]{1,0:T(8,128)(2,1)} %fusion.65, bf16[3072,768]{1,0:T(8,128)(2,1)} %all-gather.8.cloned.1.call-done), kind=kOutput, calls=%fused_computation.33 | convolution fusion | flops 5706544128 | bytes 28692480 | tf_op jit(solution)/shard_map/dot_general | solution.py:45
  264.3 13.4 %multiply_reduce_fusion.2 = (f32[768]{0:T(1024)}, f32[1200]{0:T(1024)S(1)}, f32[1200]{0:T(1024)S(1)}, f32[768]{0:T(1024)}, f32[1200,768]{1,0:T(8,128)S(1)}) fusion(f32[1200]{0:T(1024)S(1)} %add_rsqrt_fusion, f32[1200]{0:T(1024)S(1)} %broadcast_multiply_fusion.2, f32[1200,768]{1,0:T(8,128)S(1)} %copy-done.3, bf16[576,768]{1,0:T(8,128)(2,1)S(1)} %bitcast.199, ...), kind=kOutput, calls=%fused_computation.86 | convolution fusion | flops 5673365504 | bytes 20382144 | tf_op jit(solution)/shard_map/dot_general | solution.py:45
  277.7 4.1 fusion.60
  285.4 4.7 all-to-all-start.4
  291.6 6.7 all-reduce.4
  301.8 10.7 %all-to-all-done.4 = bf16[8,72,768]{2,1,0:T(8,128)(2,1)S(1)} async-done(((bf16[8,72,768]{2,1,0:T(8,128)(2,1)}), bf16[8,72,768]{2,1,0:T(8,128)(2,1)S(1)}, u32[]{:S(2)}, u32[]{:S(2)}) %all-to-all-start.4) | async-done | bytes 884768 | tf_op jit(solution)/shard_map/all_to_all | solution.py:179
  314.0 10.8 %fusion.64 = bf16[1200,768]{1,0:T(8,128)(2,1)S(1)} fusion(bf16[1200,3072]{1,0:T(8,128)(2,1)} %copy-done.72, bf16[3072,768]{1,0:T(8,128)(2,1)} %all-gather.8.cloned.1.call-done, f32[768]{0:T(1024)S(1)} %all-reduce.4, f32[1200,768]{1,0:T(8,128)} %copy-done.1, bf16[576,768]{1,0:T(8,128)(2,1)S(1)} %bitcast.201, f32[1200]{0:T(1024)S(1)} %fusion.123), kind=kOutput, calls=%fused_computation.99 | convolution fusion | flops 5667840000 | bytes 18513600 | tf_op jit(solution)/shard_map/dot_general | solution.py:37
  324.9 7.6 %collective-permute-done.3 = bf16[576,768]{1,0:T(8,128)(2,1)S(1)} collective-permute-done((bf16[576,768]{1,0:T(8,128)(2,1)S(1)}, bf16[576,768]{1,0:T(8,128)(2,1)S(1)}, u32[]{:S(2)}, u32[]{:S(2)}) %collective-permute-start.3) | collective-permute-done | bytes 884768 | tf_op jit(solution)/shard_map/ppermute | solution.py:230
  334.0 10.3 %convolution_convert_fusion.1 = bf16[768,3072]{1,0:T(8,128)(2,1)S(1)} fusion(bf16[1200,3072]{1,0:T(8,128)(2,1)} %copy-done.71, f32[768]{0:T(1024)S(1)} %get-tuple-element.24, f32[768]{0:T(1024)S(1)} %get-tuple-element.23, f32[1200]{0:T(1024)S(1)} %add_rsqrt_fusion, f32[1200]{0:T(1024)S(1)} %broadcast_multiply_fusion.2, f32[1200,768]{1,0:T(8,128)S(1)} %copy-done.4, ...), kind=kOutput, calls=%fused_computation.66 | convolution fusion | flops 5672042496 | bytes 16683072 | tf_op jit(solution)/shard_map/dot_general | solution.py:41
  344.3 2.5 copy.186
  349.5 3.6 all-to-all-start.2
  353.7 7.9 %fusion.56 = bf16[2432,192]{0,1:T(8,128)(2,1)} fusion(s32[2304]{0:T(1024)S(1)} %copy-done.51, s32[2432]{0:T(1024)S(1)} %copy-done.55, bf16[192,768]{1,0:T(8,128)(2,1)S(1)} %copy-done.28, bf16[1152,768]{1,0:T(8,128)(2,1)} %collective-permute-done.4, bf16[576,768]{1,0:T(8,128)(2,1)} %copy-done.25, bf16[576,768]{1,0:T(8,128)(2,1)S(1)} %bitcast.214), kind=kOutput, calls=%fused_computation.81 | convolution fusion | flops 2848284672 | bytes 4786688 | tf_op jit(solution)/shard_map/dot_general | solution.py:37
  361.6 3.8 reshape.354
  365.5 8.5 %fusion.75 = bf16[8,304,1,3,64]{1,4,3,0,2:T(8,128)(2,1)} fusion(bf16[8,304,3,64]{1,0,3,2:T(8,128)(2,1)} %reshape.354, f32[8,3,304,304]{2,3,1,0:T(8,128)} %get-tuple-element.66, f32[8,3,304]{2,1,0:T(4,128)} %copy-done.35), kind=kOutput, calls=%fused_computation.130 | convolution fusion | flops 288337920 | bytes 10768896 | tf_op jit(solution)/shard_map/rhqk,rqhe->rkhe/dot_general | solution.py:236
  374.0 7.5 %multiply_reduce_fusion = (f32[8,3,304]{2,1,0:T(4,128)S(1)}, f32[8,3,304,304]{2,3,1,0:T(8,128)S(1)}) fusion(f32[8,3,304,304]{2,3,1,0:T(8,128)} %get-tuple-element.66, f32[8,3,304]{2,1,0:T(4,128)S(1)} %copy-done.36, bf16[8,304,1,3,64]{1,0,4,3,2:T(8,128)(2,1)S(1)} %copy-done.21, bf16[8,304,3,64]{1,0,3,2:T(8,128)(2,1)} %reshape.354), kind=kOutput, calls=%fused_computation.40 | convolution fusion | flops 290548608 | bytes 19670016 | tf_op jit(solution)/shard_map/rqhe,rkhe->rhqk/dot_general | solution.py:235
  387.5 4.1 copy.131
  391.6 6.5 convert_element_type.200
  398.1 4.4 all-to-all-start.3
  402.6 16.6 %fusion.62 = f32[2304,768]{1,0:T(8,128)} fusion(bf16[768,576]{0,1:T(8,128)(2,1)S(1)} %bitcast.192, bf16[2432,576]{0,1:T(8,128)(2,1)} %convert_element_type.200, s32[2304]{0:T(1024)S(1)} %copy-done.52, s32[2432]{0:T(1024)S(1)} %copy-done.56), kind=kOutput, calls=%fused_computation.98 | convolution fusion | flops 8500396032 | bytes 10783232 | tf_op jit(solution)/shard_map/dot_general | solution.py:45
  419.2 3.6 slice.288
  427.9 2.4 multiply_reduce_fusion.1
  435.1 3.5 all-to-all-start.7
  442.3 13.4 %fusion.2 = f32[4616,192]{0,1:T(8,128)} fusion(bf16[2496,192]{0,1:T(8,128)(2,1)} %reshape.351, s32[4616]{0:T(1024)S(1)} %copy-done.41), kind=kOutput, calls=%fused_computation.3 | convolution fusion | flops 4435791360 | bytes 4522016 | tf_op jit(solution)/shard_map/dot_general | solution.py:37
  455.7 3.0 slice_add_fusion
  463.6 12.8 %fusion.40 = bf16[4616,192]{0,1:T(8,128)(2,1)} fusion(f32[4616,192]{0,1:T(8,128)S(1)} %copy-done.73, bf16[2304,192]{0,1:T(8,128)(2,1)S(1)} %copy-done.27, s32[4616]{0:T(1024)S(1)} %copy-done.39), kind=kOutput, calls=%fused_computation.57 | convolution fusion | flops 4096349184 | bytes 6220832 | tf_op jit(solution)/shard_map/dot_general | solution.py:37
  478.9 5.0 collective-permute-done.6
  483.9 2.8 fusion.71
  486.7 5.3 all-to-all-start.5
  494.1 6.3 convolution_convert_fusion.3
  502.0 3.1 fusion.86
  506.9 4.6 collective-permute-start.9
  511.5 2.8 all-to-all-done.5
  516.2 2.7 fusion.74
  518.9 3.0 add_convert_fusion.3
  523.3 3.7 all-to-all-start.6
  527.1 13.4 %fusion.1 = f32[4616,192]{0,1:T(8,128)} fusion(bf16[2496,192]{0,1:T(8,128)(2,1)} %reshape.359, s32[4616]{0:T(1024)S(1)} %copy-done.42), kind=kOutput, calls=%fused_computation.2 | convolution fusion | flops 4435791360 | bytes 4522016 | tf_op jit(solution)/shard_map/dot_general | solution.py:37
  541.9 40.4 %psum.37 = f32[11,768]{1,0:T(8,128)S(1)} all-reduce(f32[11,768]{1,0:T(8,128)S(1)} %concatenate.16), channel_id=1, replica_groups=mesh['tok'=8,'tp'=4] {'tok','tp'}, use_global_device_ids=true, to_apply=%region_31.32 | all-reduce | flops 8448 | bytes 67584 | tf_op jit(solution)/shard_map/psum | solution.py:274
  585.7 13.6 %fusion.39 = f32[4616,192]{0,1:T(8,128)} fusion(f32[4616,192]{0,1:T(8,128)} %fusion.1, bf16[2304,192]{0,1:T(8,128)(2,1)S(1)} %reshape.357, s32[4616]{0:T(1024)S(1)} %copy-done.40), kind=kOutput, calls=%fused_computation.56 | convolution fusion | flops 4095462912 | bytes 7993376 | tf_op jit(solution)/shard_map/dot_general | solution.py:37
  599.3 56.6 %all-reduce.8.cloned.1.call-done = (bf16[768,3,192]{0,2,1:T(8,128)(2,1)}, bf16[192,768]{1,0:T(8,128)(2,1)}, bf16[768,768]{1,0:T(8,128)(2,1)}, bf16[768,768]{1,0:T(8,128)(2,1)}) async-done(((bf16[768,3,192]{0,2,1:T(8,128)(2,1)}, bf16[192,768]{1,0:T(8,128)(2,1)}, bf16[768,768]{1,0:T(8,128)(2,1)}, bf16[768,768]{1,0:T(8,128)(2,1)}), (bf16[768,3,192]{0,2,1:T(8,128)(2,1)}, bf16[192,768]{1,0:T(8,128)(2,1)}, ...) | async-done | bytes 3538960 | tf_op jit(solution)/shard_map/psum | solution.py:250
  657.9 2.5 reshape.361
  (317 shorter events, 85.0 us)
Async XLA Ops:
  7.2 99.3 %copy-start = (bf16[768,3,192]{0,2,1:T(8,128)(2,1)S(1)}, bf16[768,3,192]{0,2,1:T(8,128)(2,1)}, u32[]{:S(2)}) copy-start(bf16[768,3,192]{0,2,1:T(8,128)(2,1)} %param.20) | copy-start | bytes 2654212
  7.2 211.3 %all-gather.6.cloned.1.call-start = ((), (), s32[]{:S(2)}) async-start(), calls=%async_computation.12 | async-start | bytes 5898240 | tf_op jit(solution)/shard_map/all_gather | solution.py:112
  8.1 23.2 %copy-start.29 = (f32[768]{0:T(1024)}, f32[768]{0:T(1024)S(1)}, u32[]{:S(2)}) copy-start(f32[768]{0:T(1024)S(1)} %get-tuple-element.21) | copy-start | bytes 9220
  32.1 49.2 %copy-start.68 = (f32[192]{0:T(256)S(1)}, f32[192]{0:T(256)}, u32[]{:S(2)}) copy-start(f32[192]{0:T(256)} %param.23) | copy-start | bytes 2308
  32.1 49.4 %copy-start.67 = (f32[2,192]{1,0:T(2,128)S(1)}, f32[2,192]{1,0:T(2,128)}, u32[]{:S(2)}) copy-start(f32[2,192]{1,0:T(2,128)} %param.21) | copy-start | bytes 4612
  80.6 3.9 collective-permute-start
  80.7 169.3 %all-gather.8.cloned.1.call-start = ((), (), s32[]{:S(2)}) async-start(), calls=%async_computation.13 | async-start | bytes 5898240 | tf_op jit(solution)/shard_map/all_gather | solution.py:113
  81.6 21.0 %copy-start.53 = (s32[2432]{0:T(1024)}, s32[2432]{0:T(1024)S(1)}, u32[]{:S(2)}) copy-start(s32[2432]{0:T(1024)S(1)} %fusion.120) | copy-start | bytes 29188
  89.7 51.7 %copy-start.50 = (s32[2304]{0:T(1024)}, s32[2304]{0:T(1024)S(1)}, u32[]{:S(2)}) copy-start(s32[2304]{0:T(1024)S(1)} %eq.201) | copy-start | bytes 27652
  149.7 3.9 collective-permute-start.1
  149.9 8.5 %copy-start.43 = (s32[4616]{0:T(1024)S(1)}, s32[4616]{0:T(1024)}, u32[]{:S(2)}) copy-start(s32[4616]{0:T(1024)} %get-tuple-element.47) | copy-start | bytes 55396
  157.0 41.9 %collective-permute-start.2 = (bf16[576,768]{1,0:T(8,128)(2,1)S(1)}, bf16[576,768]{1,0:T(8,128)(2,1)S(1)}, u32[]{:S(2)}, u32[]{:S(2)}) collective-permute-start(bf16[576,768]{1,0:T(8,128)(2,1)S(1)} %slice.292), channel_id=1, source_target_pairs={{0,2},{1,3},{2,0},{3,1},{4,6},{5,7},{6,4},{7,5},{8,10},{9,11},{10,... | collective-permute-start | bytes 2654216 | tf_op jit(solution)/shard_map/ppermute | solution.py:175
  158.4 15.2 %copy-start.64 = (f32[768]{0:T(1024)S(1)}, f32[768]{0:T(1024)}, u32[]{:S(2)}) copy-start(f32[768]{0:T(1024)} %param.26) | copy-start | bytes 9220
  158.4 15.2 %copy-start.44 = (f32[768]{0:T(1024)S(1)}, f32[768]{0:T(1024)}, u32[]{:S(2)}) copy-start(f32[768]{0:T(1024)} %param.18) | copy-start | bytes 9220
  173.5 25.4 %copy-start.63 = (f32[2,768]{1,0:T(2,128)S(1)}, f32[2,768]{1,0:T(2,128)}, u32[]{:S(2)}) copy-start(f32[2,768]{1,0:T(2,128)} %param.24) | copy-start | bytes 18436
  178.6 39.8 %copy-start.31 = (f32[1200]{0:T(1024)}, f32[1200]{0:T(1024)S(1)}, u32[]{:S(2)}) copy-start(f32[1200]{0:T(1024)S(1)} %convolution_reduce_fusion) | copy-start | bytes 14404
  200.0 26.5 %all-to-all-start.1 = ((bf16[8,72,768]{2,1,0:T(8,128)(2,1)}), bf16[8,72,768]{2,1,0:T(8,128)(2,1)S(1)}, u32[]{:S(2)}, u32[]{:S(2)}) async-start(bf16[8,72,768]{2,1,0:T(8,128)(2,1)} %bitcast.21), calls=%async_computation.1 | async-start | bytes 1769472 | tf_op jit(solution)/shard_map/all_to_all | solution.py:179
  203.6 312.5 %reduce-scatter.5.cloned.1.call-start = ((), (), s32[]{:S(2)}) async-start(), calls=%async_computation.11 | async-start | bytes 5898240 | tf_op jit(solution)/shard_map/reduce_scatter | solution.py:226
  231.1 10.5 %copy-start.19 = (bf16[1200,768]{1,0:T(8,128)(2,1)S(1)}, bf16[1200,768]{1,0:T(8,128)(2,1)}, u32[]{:S(2)}) copy-start(bf16[1200,768]{1,0:T(8,128)(2,1)} %fusion.65) | copy-start | bytes 5529604
  250.0 14.4 %copy-start.3 = (f32[1200,768]{1,0:T(8,128)S(1)}, f32[1200,768]{1,0:T(8,128)}, u32[]{:S(2)}) copy-start(f32[1200,768]{1,0:T(8,128)} %copy-done.1) | copy-start | bytes 11059204
  264.3 13.4 %copy-start.71 = (bf16[1200,3072]{1,0:T(8,128)(2,1)}, bf16[1200,3072]{1,0:T(8,128)(2,1)S(1)}, u32[]{:S(2)}) copy-start(bf16[1200,3072]{1,0:T(8,128)(2,1)S(1)} %get-tuple-element.73) | copy-start | bytes 22118404
  264.3 13.4 %copy-start.20 = (bf16[1200,768]{1,0:T(8,128)(2,1)S(1)}, bf16[1200,768]{1,0:T(8,128)(2,1)}, u32[]{:S(2)}) copy-start(bf16[1200,768]{1,0:T(8,128)(2,1)} %fusion.65) | copy-start | bytes 5529604
  281.9 9.5 %copy-start.69 = (f32[192]{0:T(256)S(1)}, f32[192]{0:T(256)}, u32[]{:S(2)}) copy-start(f32[192]{0:T(256)} %param.28) | copy-start | bytes 2308
  285.4 27.0 %all-to-all-start.4 = ((bf16[8,72,768]{2,1,0:T(8,128)(2,1)}), bf16[8,72,768]{2,1,0:T(8,128)(2,1)S(1)}, u32[]{:S(2)}, u32[]{:S(2)}) async-start(bf16[8,72,768]{2,1,0:T(8,128)(2,1)} %bitcast.32), calls=%async_computation.4 | async-start | bytes 1769472 | tf_op jit(solution)/shard_map/all_to_all | solution.py:179
  312.4 20.0 %copy-start.14 = (bf16[8,72,768]{2,1,0:T(8,128)(2,1)}, bf16[8,72,768]{2,1,0:T(8,128)(2,1)S(1)}, u32[]{:S(2)}) copy-start(bf16[8,72,768]{2,1,0:T(8,128)(2,1)S(1)} %all-to-all-done.4) | copy-start | bytes 2654212
  312.5 20.0 %collective-permute-start.3 = (bf16[576,768]{1,0:T(8,128)(2,1)S(1)}, bf16[576,768]{1,0:T(8,128)(2,1)S(1)}, u32[]{:S(2)}, u32[]{:S(2)}) collective-permute-start(bf16[576,768]{1,0:T(8,128)(2,1)S(1)} %bitcast.212), channel_id=1, source_target_pairs={{0,2},{1,3},{2,0},{3,1},{4,6},{5,7},{6,4},{7,5},{8,10},{9,11},{10,... | collective-permute-start | bytes 2654216 | tf_op jit(solution)/shard_map/ppermute | solution.py:230
  324.8 9.0 %copy-start.13 = (bf16[1200,768]{1,0:T(8,128)(2,1)}, bf16[1200,768]{1,0:T(8,128)(2,1)S(1)}, u32[]{:S(2)}) copy-start(bf16[1200,768]{1,0:T(8,128)(2,1)S(1)} %fusion.64) | copy-start | bytes 5529604
  324.8 9.1 %copy-start.4 = (f32[1200,768]{1,0:T(8,128)S(1)}, f32[1200,768]{1,0:T(8,128)}, u32[]{:S(2)}) copy-start(f32[1200,768]{1,0:T(8,128)} %copy-done.1) | copy-start | bytes 11059204
  334.0 19.7 %collective-permute-start.4 = (bf16[1152,768]{1,0:T(8,128)(2,1)}, bf16[1152,768]{1,0:T(8,128)(2,1)}, u32[]{:S(2)}, u32[]{:S(2)}) collective-permute-start(bf16[1152,768]{1,0:T(8,128)(2,1)} %pad_maximum_fusion.2), channel_id=1, source_target_pairs={{0,1},{1,0},{2,3},{3,2},{4,5},{5,4},{6,7},{7,6},{8,9},{9,8},{10,11... | collective-permute-start | bytes 5308424 | tf_op jit(solution)/shard_map/ppermute | solution.py:231
  349.5 48.7 %all-to-all-start.2 = ((bf16[4,576,192]{1,2,0:T(8,128)(2,1)}), bf16[4,576,192]{1,2,0:T(8,128)(2,1)S(1)}, u32[]{:S(2)}, u32[]{:S(2)}) async-start(bf16[4,576,192]{1,2,0:T(8,128)(2,1)} %bitcast.29), calls=%async_computation.2 | async-start | bytes 1966080 | tf_op jit(solution)/shard_map/all_to_all | solution.py:262
  353.1 163.0 %reduce-scatter.3.cloned.1.call-start = ((), (), s32[]{:S(2)}) async-start(), calls=%async_computation.10 | async-start | bytes 5898240 | tf_op jit(solution)/shard_map/reduce_scatter | solution.py:225
  365.5 8.5 %copy-start.21 = (bf16[8,304,1,3,64]{1,0,4,3,2:T(8,128)(2,1)S(1)}, bf16[8,304,1,3,64]{1,0,4,3,2:T(8,128)(2,1)}, u32[]{:S(2)}) copy-start(bf16[8,304,1,3,64]{1,0,4,3,2:T(8,128)(2,1)} %get-tuple-element.39) | copy-start | bytes 2801668
  365.5 8.5 %copy-start.36 = (f32[8,3,304]{2,1,0:T(4,128)S(1)}, f32[8,3,304]{2,1,0:T(4,128)}, u32[]{:S(2)}) copy-start(f32[8,3,304]{2,1,0:T(4,128)} %copy-done.35) | copy-start | bytes 87556
  365.5 16.0 %slice-start = ((s8[11206656]{0:T(1024)(128)(4,1)}), s8[4194304]{0:T(1024)(128)(4,1)S(1)}, s32[]{:S(2)}) async-start(s8[11206656]{0:T(1024)(128)(4,1)} %bitcast.203), calls=%async_computation.15 | async-start | bytes 8388608
  365.5 16.0 %slice-start.1 = ((s8[11206656]{0:T(1024)(128)(4,1)}), s8[4194304]{0:T(1024)(128)(4,1)S(1)}, s32[]{:S(2)}) async-start(s8[11206656]{0:T(1024)(128)(4,1)} %bitcast.203), calls=%async_computation.16 | async-start | bytes 8388608
  391.6 11.0 %copy-start.52 = (s32[2304]{0:T(1024)S(1)}, s32[2304]{0:T(1024)}, u32[]{:S(2)}) copy-start(s32[2304]{0:T(1024)} %copy-done.50) | copy-start | bytes 27652
  391.6 11.0 %copy-start.56 = (s32[2432]{0:T(1024)S(1)}, s32[2432]{0:T(1024)}, u32[]{:S(2)}) copy-start(s32[2432]{0:T(1024)} %copy-done.53) | copy-start | bytes 29188
  398.1 37.0 %all-to-all-start.3 = ((bf16[4,624,192]{1,2,0:T(8,128)(2,1)}), bf16[4,624,192]{1,2,0:T(8,128)(2,1)}, u32[]{:S(2)}, u32[]{:S(2)}) async-start(bf16[4,624,192]{1,2,0:T(8,128)(2,1)} %bitcast.31), calls=%async_computation.3 | async-start | bytes 1966080 | tf_op jit(solution)/shard_map/all_to_all | solution.py:262
  419.1 8.7 %copy-start.32 = (f32[1200]{0:T(1024)S(1)}, f32[1200]{0:T(1024)}, u32[]{:S(2)}) copy-start(f32[1200]{0:T(1024)} %copy-done.31) | copy-start | bytes 14404
  419.1 8.7 %copy-start.38 = (f32[1200]{0:T(1024)S(1)}, f32[1200]{0:T(1024)}, u32[]{:S(2)}) copy-start(f32[1200]{0:T(1024)} %get-tuple-element.33) | copy-start | bytes 14404
  422.8 33.0 %collective-permute-start.5 = (bf16[1152,768]{1,0:T(8,128)(2,1)}, bf16[1152,768]{1,0:T(8,128)(2,1)}, u32[]{:S(2)}, u32[]{:S(2)}) collective-permute-start(bf16[1152,768]{1,0:T(8,128)(2,1)} %slice.288), channel_id=1, source_target_pairs={{0,1},{1,0},{2,3},{3,2},{4,5},{5,4},{6,7},{7,6},{8,9},{9,8},{10,11... | collective-permute-start | bytes 5308424 | tf_op jit(solution)/shard_map/ppermute | solution.py:173
  433.5 8.8 %copy-start.41 = (s32[4616]{0:T(1024)S(1)}, s32[4616]{0:T(1024)}, u32[]{:S(2)}) copy-start(s32[4616]{0:T(1024)} %get-tuple-element.49) | copy-start | bytes 55396
  435.1 41.2 %all-to-all-start.7 = ((bf16[4,624,192]{1,2,0:T(8,128)(2,1)}), bf16[4,624,192]{1,2,0:T(8,128)(2,1)S(1)}, u32[]{:S(2)}, u32[]{:S(2)}) async-start(bf16[4,624,192]{1,2,0:T(8,128)(2,1)} %bitcast.211), calls=%async_computation.7 | async-start | bytes 1966080 | tf_op jit(solution)/shard_map/all_to_all | solution.py:262
  461.6 22.3 %collective-permute-start.6 = (bf16[576,768]{1,0:T(8,128)(2,1)}, bf16[576,768]{1,0:T(8,128)(2,1)}, u32[]{:S(2)}, u32[]{:S(2)}) collective-permute-start(bf16[576,768]{1,0:T(8,128)(2,1)} %slice.291), channel_id=1, source_target_pairs={{0,2},{1,3},{2,0},{3,1},{4,6},{5,7},{6,4},{7,5},{8,10},{9,11},{10,... | collective-permute-start | bytes 2654216 | tf_op jit(solution)/shard_map/ppermute | solution.py:175
  486.7 27.7 %all-to-all-start.5 = ((bf16[8,72,768]{2,1,0:T(8,128)(2,1)}), bf16[8,72,768]{2,1,0:T(8,128)(2,1)S(1)}, u32[]{:S(2)}, u32[]{:S(2)}) async-start(bf16[8,72,768]{2,1,0:T(8,128)(2,1)} %bitcast.40), calls=%async_computation.5 | async-start | bytes 1769472 | tf_op jit(solution)/shard_map/all_to_all | solution.py:179
  492.0 163.9 %all-reduce.8.cloned.1.call-start = ((), (), s32[]{:S(2)}) async-start(), calls=%async_computation.14 | async-start | bytes 7077888 | tf_op jit(solution)/shard_map/psum | solution.py:250
  492.1 9.9 %copy-start.16 = (bf16[8,72,768]{2,1,0:T(8,128)(2,1)S(1)}, bf16[8,72,768]{2,1,0:T(8,128)(2,1)}, u32[]{:S(2)}) copy-start(bf16[8,72,768]{2,1,0:T(8,128)(2,1)} %copy-done.14) | copy-start | bytes 2654212
  492.1 9.9 %copy-start.18 = (bf16[2304,192]{0,1:T(8,128)(2,1)S(1)}, bf16[2304,192]{0,1:T(8,128)(2,1)}, u32[]{:S(2)}) copy-start(bf16[2304,192]{0,1:T(8,128)(2,1)} %copy-done.17) | copy-start | bytes 2654212
  492.1 9.9 %copy-start.26 = (bf16[576,768]{1,0:T(8,128)(2,1)S(1)}, bf16[576,768]{1,0:T(8,128)(2,1)}, u32[]{:S(2)}) copy-start(bf16[576,768]{1,0:T(8,128)(2,1)} %copy-done.25) | copy-start | bytes 2654212
  492.1 8.3 %collective-permute-start.7 = (f32[2,192]{1,0:T(2,128)S(1)}, f32[2,192]{1,0:T(2,128)S(1)}, u32[]{:S(2)}, u32[]{:S(2)}) collective-permute-start(f32[2,192]{1,0:T(2,128)S(1)} %pad_maximum_fusion.8), channel_id=1, source_target_pairs={{0,4},{4,0},{8,12},{12,8},{16,20},{20,16},{24,28},{28,24},{1,5},{5... | collective-permute-start | bytes 4616 | tf_op jit(solution)/shard_map/ppermute | solution.py:279
  500.4 13.9 %copy-start.30 = (f32[768]{0:T(1024)S(1)}, f32[768]{0:T(1024)}, u32[]{:S(2)}) copy-start(f32[768]{0:T(1024)} %copy-done.29) | copy-start | bytes 9220
  500.4 5.9 collective-permute-start.8
  505.0 11.1 %copy-start.37 = (f32[576]{0:T(1024)S(1)}, f32[576]{0:T(1024)}, u32[]{:S(2)}) copy-start(f32[576]{0:T(1024)} %add_rsqrt_fusion.2) | copy-start | bytes 6916
  506.9 33.6 %collective-permute-start.9 = (f32[2,192]{1,0:T(2,128)}, f32[2,192]{1,0:T(2,128)}, u32[]{:S(2)}, u32[]{:S(2)}) collective-permute-start(f32[2,192]{1,0:T(2,128)} %fusion.173), channel_id=1, source_target_pairs={{0,16},{4,20},{8,24},{12,28},{16,0},{20,4},{24,8},{28,12},{1,17},{... | collective-permute-start | bytes 4616 | tf_op jit(solution)/shard_map/ppermute | solution.py:279
  523.3 61.0 %all-to-all-start.6 = ((bf16[4,576,192]{1,2,0:T(8,128)(2,1)}), bf16[4,576,192]{1,2,0:T(8,128)(2,1)S(1)}, u32[]{:S(2)}, u32[]{:S(2)}) async-start(bf16[4,576,192]{1,2,0:T(8,128)(2,1)} %bitcast.43), calls=%async_computation.6 | async-start | bytes 1966080 | tf_op jit(solution)/shard_map/all_to_all | solution.py:262
  527.0 14.8 %copy-start.47 = (f32[768]{0:T(1024)S(1)}, f32[768]{0:T(1024)}, u32[]{:S(2)}) copy-start(f32[768]{0:T(1024)} %get-tuple-element.19) | copy-start | bytes 9220
  527.0 14.8 %copy-start.49 = (f32[768]{0:T(1024)S(1)}, f32[768]{0:T(1024)}, u32[]{:S(2)}) copy-start(f32[768]{0:T(1024)} %get-tuple-element.15) | copy-start | bytes 9220
  527.0 14.8 %copy-start.34 = (f32[4,768]{1,0:T(4,128)S(1)}, f32[4,768]{1,0:T(4,128)}, u32[]{:S(2)}) copy-start(f32[4,768]{1,0:T(4,128)} %reshape.362) | copy-start | bytes 36868
  527.0 14.8 %copy-start.58 = (f32[1,768]{1,0:T(1,128)S(1)}, f32[1,768]{1,0:T(1,128)}, u32[]{:S(2)}) copy-start(f32[1,768]{1,0:T(1,128)} %stack.69) | copy-start | bytes 9220
  527.0 14.8 %copy-start.59 = (f32[1,768]{1,0:T(1,128)S(1)}, f32[1,768]{1,0:T(1,128)}, u32[]{:S(2)}) copy-start(f32[1,768]{1,0:T(1,128)} %stack.70) | copy-start | bytes 9220
  527.0 14.8 %copy-start.60 = (f32[1,768]{1,0:T(1,128)S(1)}, f32[1,768]{1,0:T(1,128)}, u32[]{:S(2)}) copy-start(f32[1,768]{1,0:T(1,128)} %stack.71) | copy-start | bytes 9220
  527.0 14.8 %copy-start.61 = (f32[1,768]{1,0:T(1,128)S(1)}, f32[1,768]{1,0:T(1,128)}, u32[]{:S(2)}) copy-start(f32[1,768]{1,0:T(1,128)} %stack.73) | copy-start | bytes 9220
  527.0 14.8 %copy-start.62 = (f32[1,768]{1,0:T(1,128)S(1)}, f32[1,768]{1,0:T(1,128)}, u32[]{:S(2)}) copy-start(f32[1,768]{1,0:T(1,128)} %stack.72) | copy-start | bytes 9220
  540.5 45.2 %copy-start.40 = (s32[4616]{0:T(1024)S(1)}, s32[4616]{0:T(1024)}, u32[]{:S(2)}) copy-start(s32[4616]{0:T(1024)} %get-tuple-element.45) | copy-start | bytes 55396
  (38 other events, 179.9 us)
Sparse Core Ops, SparseCore 0:
  80.8 36.5 all-gather.5
  150.0 55.4 all-gather.7
  250.0 47.8 reduce-scatter.4
  356.3 48.7 reduce-scatter.2
  516.3 139.6 all-reduce.7
